TPU v7x, 128 devices: a whole 4x4x4 slice. The times are simulated.
128 devices in a mesh: lat: 8 (over z, core), lon: 16 (over y, x).
Axes of the slice: x: 4, y: 4, z: 4, core: 2. Of those that a mesh axis runs over, the one named last changes fastest.
Arguments:
- control: float32 [254, 64, 1536], P(None, 'lat', 'lon'), may hold values from -6 to 6
- vert_band: float32 [2, 9, 127], replicated, may hold values from -2.5 to 2.5
- lat_length: float32 [254, 8], replicated, may hold values from 3 to 32
- lon_length: float32 [254], replicated, may hold values from 3 to 192
- band_index: int32 [64], replicated, may hold values from 0 to 7
- owner_device: int32 [254, 1], replicated, may hold values from 0 to 127; in each aligned block of 254 rows (0 to 253, 254 to 507, ...) at most 4 rows name the same one
Outputs:
- winds: float32 [254, 64, 1536], P(None, 'lat', 'lon')
- slabs: float32 [512, 64, 1536], P(('lat', 'lon'))
Inputs may be any that keep to these rules, and one draw needn't show every extreme that they name: owner_device[s, 0] numbers a device along the joined axes lat+lon; no device owns more than 4 level-variables, one owns exactly 4, and every device owns at least one.
All inputs are finite; a program needn't handle non-finite values.
Results may differ from a plain program's by a relative error of at most 0.0003.
Values sent between devices are 32-bit elements; how exact they have to be, the bound alone decides.
A program may use at most 64 MiB of HBM per device.

v0:
```python
import math
import jax
import jax.numpy as jnp
from jax import lax
from jax.sharding import PartitionSpec as P

NLAT_GLOBE = 768
HIGH_ACCURACY = lax.Precision.HIGHEST


def padded(block, sides, width, periodic):
    for axis, dim in sides:
        count = lax.axis_size(axis)
        forward = [(i, i + 1) for i in range(count - 1)]
        if periodic:
            forward.append((count - 1, 0))
        backward = [(target, source) for source, target in forward]
        low = lax.ppermute(
            lax.slice_in_dim(block, block.shape[dim] - width, None, axis=dim), axis, forward
        )
        high = lax.ppermute(lax.slice_in_dim(block, 0, width, axis=dim), axis, backward)
        block = jnp.concatenate([low, block, high], axis=dim)
    return block


def slot_sources(owner_device, devices_all, most_slots):
    owners = owner_device[:, 0]
    level_ids = jnp.arange(owners.shape[0], dtype=jnp.int32)
    sharing = (owners[:, None] == owners[None, :]) & (level_ids[None, :] < level_ids[:, None])
    rank_in = jnp.sum(sharing.astype(jnp.int32), axis=1)
    slot_of = owners * most_slots + rank_in
    slot_numbers = jnp.arange(devices_all * most_slots, dtype=jnp.int32)
    matches = slot_of[None, :] == slot_numbers[:, None]
    filled = jnp.any(matches, axis=1)
    source = jnp.argmax(matches.astype(jnp.int32), axis=1)
    return (owners, rank_in, source, filled)


def rate_tables(inverse, block_len):
    slab_total, length = inverse.shape
    blocks = length // block_len
    decays = jnp.exp(-inverse)
    weights = jnp.sqrt(1.0 - decays * decays).reshape(slab_total, blocks, block_len)
    logsum = jnp.cumsum(-inverse.reshape(slab_total, blocks, block_len), axis=2)
    within = jnp.arange(block_len)
    below = within[:, None] >= within[None, :]
    spread = jnp.minimum(logsum[:, :, :, None] - logsum[:, :, None, :], 0.0)
    transfer = jnp.where(below, jnp.exp(spread), 0.0) * weights[:, :, None, :]
    return (transfer, jnp.exp(logsum))


def block_carries(gains, ends):

    def advance(running, inputs):
        gain, tail = inputs
        return (gain[:, None] * running + tail, running)

    initial = jnp.zeros_like(ends[:, 0])
    _, entries = lax.scan(advance, initial, (gains.T, jnp.moveaxis(ends, 1, 0)))
    return jnp.moveaxis(entries, 0, 1)


def sweep_rows(fields, transfer, reach):
    slab_total, length, across = fields.shape
    blocks, block_len = (reach.shape[1], reach.shape[2])
    parts = fields.reshape(slab_total, blocks, block_len, across)
    local = jnp.einsum("sbnm,sbmw->sbnw", transfer, parts, precision=HIGH_ACCURACY)
    entries = block_carries(reach[:, :, -1], local[:, :, -1, :])
    result = local + reach[:, :, :, None] * entries[:, :, None, :]
    return result.reshape(slab_total, length, across)


def sweep_cols(fields, transfer, reach):
    slab_total, across, length = fields.shape
    blocks, block_len = (reach.shape[1], reach.shape[2])
    parts = fields.reshape(slab_total, across, blocks, block_len)
    local = jnp.einsum("sbnm,swbm->swbn", transfer, parts, precision=HIGH_ACCURACY)
    entries = block_carries(reach[:, :, -1], jnp.swapaxes(local[:, :, :, -1], 1, 2))
    result = local + reach[:, None, :, :] * jnp.swapaxes(entries, 1, 2)[:, :, :, None]
    return result.reshape(slab_total, across, length)


def filter_slabs(slab, lat_inverse, lon_inverse):
    slot_total, lat_full, lon_full = slab.shape
    lat_block = math.gcd(lat_full, 128)
    lat_mats, lat_reach = rate_tables(lat_inverse, lat_block)
    northward = sweep_rows(slab, lat_mats, lat_reach)
    back_mats, back_reach = rate_tables(jnp.flip(lat_inverse, 1), lat_block)
    southward = jnp.flip(sweep_rows(jnp.flip(northward, 1), back_mats, back_reach), 1)
    lon_block = math.gcd(lon_full, 128)
    lon_table = jnp.broadcast_to(lon_inverse[:, None], (slot_total, lon_full))
    lon_mats, lon_reach = rate_tables(lon_table, lon_block)
    places = jnp.arange(lon_full, dtype=jnp.float32)
    closing = 1.0 / (1.0 - jnp.exp(-lon_full * lon_inverse))
    eastward = sweep_cols(southward, lon_mats, lon_reach)
    eastward = eastward + jnp.exp(-(places[None, :] + 1.0) * lon_inverse[:, None])[:, None, :] * (
        eastward[:, :, -1:] * closing[:, None, None]
    )
    westward = jnp.flip(sweep_cols(jnp.flip(eastward, 2), lon_mats, lon_reach), 2)
    westward = westward + jnp.exp(-(lon_full - places[None, :]) * lon_inverse[:, None])[
        :, None, :
    ] * (westward[:, :, :1] * closing[:, None, None])
    return westward


def to_owners(columns, source, filled, most_slots, lat_count, lon_count):
    level_vars, latitude_points, longitude_points = columns.shape
    devices_all = lat_count * lon_count
    by_slot = source.reshape(devices_all, most_slots).T.reshape(-1)
    live_slot = filled.reshape(devices_all, most_slots).T.reshape(-1)
    packed = jnp.where(live_slot[:, None, None], jnp.take(columns, by_slot, axis=0), 0.0)
    moved = lax.all_to_all(
        packed.reshape(most_slots, devices_all, latitude_points, longitude_points),
        ("lat", "lon"),
        split_axis=1,
        concat_axis=1,
        tiled=True,
    )
    moved = moved.reshape(most_slots, lat_count, lon_count, latitude_points, longitude_points)
    return moved.transpose(0, 1, 3, 2, 4).reshape(
        most_slots, lat_count * latitude_points, lon_count * longitude_points
    )


def into_columns(slab, owners, rank_in, lat_count, lon_count, latitude_points, longitude_points):
    most_slots = slab.shape[0]
    devices_all = lat_count * lon_count
    pieces = slab.reshape(
        most_slots, lat_count, latitude_points, lon_count, longitude_points
    ).transpose(0, 1, 3, 2, 4)
    returned = lax.all_to_all(
        pieces.reshape(most_slots, devices_all, latitude_points, longitude_points),
        ("lat", "lon"),
        split_axis=1,
        concat_axis=1,
        tiled=True,
    )
    flat_slots = returned.reshape(most_slots * devices_all, latitude_points, longitude_points)
    return jnp.take(flat_slots, rank_in * devices_all + owners, axis=0)


def winds_from(filtered, lat_pos, lat_full):
    level_vars, latitude_points, longitude_points = filtered.shape
    level_count_total = level_vars // 2
    lat_ext = padded(filtered, (("lat", 1),), 1, False)
    lon_ext = padded(filtered, (("lon", 2),), 1, True)
    d_lat = (lat_ext[:, 2:, :] - lat_ext[:, :-2, :]) * 0.5
    d_lon = (lon_ext[:, :, 2:] - lon_ext[:, :, :-2]) * 0.5
    latitude_rows = (lat_pos * latitude_points + jnp.arange(latitude_points)).astype(
        jnp.float32
    ) + float(NLAT_GLOBE - lat_full)
    latitude = jnp.pi * ((latitude_rows + 0.5) / NLAT_GLOBE - 0.5)
    metric = (1.0 / jnp.maximum(jnp.cos(latitude), 0.2))[None, :, None]
    east_wind = -d_lat[:level_count_total] + d_lon[level_count_total:] * metric
    north_wind = d_lon[:level_count_total] * metric + d_lat[level_count_total:]
    return jnp.concatenate([east_wind, north_wind], axis=0)


def shards(control, vert_band, lat_length, lon_length, band_index, owner_device):
    level_vars, latitude_points, longitude_points = control.shape
    lat_count = lax.axis_size("lat")
    lon_count = lax.axis_size("lon")
    devices_all = lat_count * lon_count
    most_slots = 2 * ((level_vars + devices_all - 1) // devices_all)
    lat_full = latitude_points * lat_count
    lat_pos = lax.axis_index("lat")
    lon_pos = lax.axis_index("lon")
    my_device = lat_pos * lon_count + lon_pos
    level_count_total = level_vars // 2
    band_width = vert_band.shape[1]
    half_band = band_width // 2
    diagonals = jnp.stack(
        [
            jnp.eye(level_count_total, k=offset - half_band, dtype=jnp.float32)
            for offset in range(band_width)
        ]
    )
    band_matrices = jnp.eye(level_count_total, dtype=jnp.float32)[None] + jnp.einsum(
        "vok,okl->vkl", vert_band, diagonals, precision=HIGH_ACCURACY
    )
    mixed = jnp.einsum(
        "jme,jet->jmt",
        band_matrices,
        control.reshape(2, level_count_total, latitude_points * longitude_points),
        precision=HIGH_ACCURACY,
    )
    mixed = mixed.reshape(level_vars, latitude_points, longitude_points)
    band_onehot = (
        band_index[None, :] == jnp.arange(lat_length.shape[1], dtype=jnp.int32)[:, None]
    ).astype(jnp.float32)
    lat_inverse = 1.0 / jnp.dot(lat_length, band_onehot, precision=HIGH_ACCURACY)
    lon_inverse = 1.0 / lon_length
    owners, rank_in, source, filled = slot_sources(owner_device, devices_all, most_slots)
    slab = to_owners(mixed, source, filled, most_slots, lat_count, lon_count)
    my_sources = lax.dynamic_slice_in_dim(source, my_device * most_slots, most_slots)
    slab_lat = jnp.take(lat_inverse, my_sources, axis=0)
    slab_lon = jnp.take(lon_inverse, my_sources, axis=0)
    slabs = filter_slabs(slab, slab_lat, slab_lon)
    filtered = into_columns(
        slabs, owners, rank_in, lat_count, lon_count, latitude_points, longitude_points
    )
    winds = winds_from(filtered, lat_pos, lat_full)
    return (winds, slabs)


def solution(mesh):
    placed = (P(None, "lat", "lon"), P(), P(), P(), P(), P())
    return jax.shard_map(
        shards,
        mesh=mesh,
        in_specs=placed,
        out_specs=(P(None, "lat", "lon"), P(("lat", "lon"), None, None)),
        check_vma=False,
    )
```

profile of v0, /device:TPU:1, one launch (start us, length us, event | category | flops | bytes accessed | tf_op | source)
XLA Modules:
  0.0 158.4 jit_solution(12169647411586467668)
XLA Ops:
  0.7 0.9 convert_reduce_fusion
  5.0 1.7 %reshape.571 = f32[2,127,768]{1,0,2:T(2,128)S(1)} reshape(f32[254,8,96]{0,2,1:T(8,128)} %param.10) | data formatting | bytes 1560576 | tf_op jit(solution)/shard_map/reshape | solution.py:184
  7.7 2.8 %stack.5 = pred[9,127,127]{2,0,1:T(8,128)(4,1)S(1)} concatenate(pred[1,127,127]{2,0,1:T(4,128)(4,1)S(1)} %iota_compare_fusion.12, pred[1,127,127]{2,0,1:T(4,128)(4,1)S(1)} %get-tuple-element.235, pred[1,127,127]{2,0,1:T(4,128)(4,1)S(1)} %get-tuple-element.234, pred[1,127,127]{2,0,1:T(4,128)(4,1)S(1)} %get-tuple-element.233, pred[1,127,127]{2,0,1:T(4,128)(4,1)S(1)} %get-tuple-element.232, ...), dimensions={0} | concatenate | bytes 290322 | tf_op jit(solution)/shard_map/stack | solution.py:172
  12.5 1.9 %gather_fusion.1 = f32[512,8,96]{2,1,0:T(8,128)S(1)} fusion(f32[254,8,96]{2,1,0:T(8,128)S(1)} %reshape.618, s32[1024]{0:T(1024)S(1)} %pad_clamp_fusion.1), kind=kCustom, calls=%fused_computation.1 | custom fusion | bytes 3147776 | tf_op jit(solution)/shard_map/jit(_take)/gather | solution.py:111
  14.4 2.7 %fusion.4 = f32[4,128,8,96]{3,2,0,1:T(8,128)} fusion(f32[4,128,8,96]{3,2,1,0:T(8,128)S(1)} %bitcast.98, pred[4,128]{0,1:T(8,128)(4,1)S(1)} %compare_and_fusion, pred[4,128]{0,1:T(8,128)(4,1)S(1)} %bitcast.104), kind=kLoop, calls=%fused_computation.18 | loop fusion | flops 786432 | bytes 3146752 | tf_op jit(solution)/shard_map/jit(_where)/select_n | solution.py:111
  17.0 11.5 %all-to-all-start = ((f32[4,128,8,96]{3,2,0,1:T(8,128)}), f32[4,128,8,96]{3,2,0,1:T(8,128)S(1)}, u32[]{:S(2)}, u32[]{:S(2)}) async-start(f32[4,128,8,96]{3,2,0,1:T(8,128)} %fusion.4), calls=%async_computation | async-start | bytes 4194304 | tf_op jit(solution)/shard_map/all_to_all | solution.py:112
  30.5 1.1 reduce_window_sum.30
  32.6 25.6 %all-to-all-done = f32[4,128,8,96]{3,2,0,1:T(8,128)S(1)} async-done(((f32[4,128,8,96]{3,2,0,1:T(8,128)}), f32[4,128,8,96]{3,2,0,1:T(8,128)S(1)}, u32[]{:S(2)}, u32[]{:S(2)}) %all-to-all-start) | async-done | bytes 1572896 | tf_op jit(solution)/shard_map/all_to_all | solution.py:112
  58.2 1.3 copy-done.1
  59.6 2.8 %copy.100 = f32[4,8,8,16,96]{4,3,2,1,0:T(8,128)S(1)} copy(f32[4,8,8,16,96]{4,2,0,3,1:T(8,128)} %bitcast.97) | data formatting | bytes 3145728 | tf_op jit(solution)/shard_map/transpose | solution.py:120
  62.4 2.1 %reshape.575 = f32[4,64,1536]{2,1,0:T(8,128)} reshape(f32[4,8,8,16,96]{4,3,2,1,0:T(8,128)S(1)} %copy.100) | data formatting | bytes 3145728 | tf_op jit(solution)/shard_map/reshape.12
  64.5 2.9 %convolution_add_fusion.1 = f32[4,64,1536]{2,1,0:T(8,128)S(1)} fusion(f32[4,64,1536]{2,1,0:T(8,128)} %reshape.575, f32[4,64]{1,0:T(4,128)S(1)} %exponential_multiply_fusion.1, f32[4,64]{1,0:T(4,128)S(1)} %get-tuple-element.208, f32[4,64]{1,0:T(4,128)S(1)} %reduce_window_sum.29, pred[64,64]{1,0:T(8,128)(4,1)S(1)} %iota_compare_fusion.13), kind=kOutput, calls=%fused_computation.16 | convolution fusion | flops 302448640 | bytes 3152896 | tf_op jit(solution)/shard_map/sbnm,sbmw->sbnw/dot_general | solution.py:67
  67.9 1.5 convolution_add_fusion
  69.5 4.2 %reverse.8 = f32[4,64,1536]{2,1,0:T(8,128)} reverse(f32[4,64,1536]{2,1,0:T(8,128)S(1)} %convolution_add_fusion), dimensions={1} | reverse | bytes 3145728 | tf_op jit(solution)/shard_map/reverse.2
  73.6 7.6 %fusion.19 = f32[4,64,12,128]{3,1,2,0:T(8,128)S(1)} fusion(f32[4]{0:T(128)S(1)} %get-tuple-element.227, f32[4,12,128]{2,1,0:T(8,128)S(1)} %reduce_window_sum.30, pred[128,128]{1,0:T(8,128)(4,1)S(1)} %iota_compare_fusion.2, f32[4,64,1536]{2,1,0:T(8,128)} %reverse.8), kind=kOutput, calls=%fused_computation.39 | convolution fusion | flops 607125504 | bytes 3186704 | tf_op jit(solution)/shard_map/sbnm,swbm->swbn/dot_general | solution.py:77
  82.2 1.4 while.6
  84.8 1.4 rev.15
  86.3 6.2 %fusion.22 = f32[4,64,12,128]{3,1,2,0:T(8,128)S(1)} fusion(f32[4]{0:T(128)S(1)} %get-tuple-element.227, f32[4,12,128]{2,1,0:T(8,128)S(1)} %reduce_window_sum.30, pred[128,128]{1,0:T(8,128)(4,1)S(1)} %iota_compare_fusion.2, f32[4,64,1536]{2,1,0:T(8,128)S(1)} %rev.15), kind=kOutput, calls=%fused_computation.40 | convolution fusion | flops 607125504 | bytes 3186704 | tf_op jit(solution)/shard_map/sbnm,swbm->swbn/dot_general | solution.py:77
  93.5 1.2 while.7
  95.4 1.4 rev.16
  96.8 1.4 multiply_add_fusion
  98.2 1.9 %reshape.581 = f32[4,8,8,16,96]{4,3,2,1,0:T(8,128)S(1)} reshape(f32[4,64,1536]{2,1,0:T(8,128)} %multiply_add_fusion) | data formatting | bytes 3145728 | tf_op jit(solution)/shard_map/reshape | solution.py:128
  101.0 1.6 %copy.112 = f32[4,128,8,96]{3,2,0,1:T(8,128)} copy(f32[4,128,8,96]{3,2,1,0:T(8,128)S(1)} %bitcast.99) | data formatting | bytes 3145728 | tf_op jit(solution)/shard_map/reshape | solution.py:132
  102.6 4.8 %all-to-all-start.1 = ((f32[4,128,8,96]{3,2,0,1:T(8,128)}), f32[4,128,8,96]{3,2,0,1:T(8,128)S(1)}, u32[]{:S(2)}, u32[]{:S(2)}) async-start(f32[4,128,8,96]{3,2,0,1:T(8,128)} %copy.112), calls=%async_computation.1 | async-start | bytes 4194304 | tf_op jit(solution)/shard_map/all_to_all | solution.py:131
  107.5 29.7 %all-to-all-done.1 = f32[4,128,8,96]{3,2,0,1:T(8,128)S(1)} async-done(((f32[4,128,8,96]{3,2,0,1:T(8,128)}), f32[4,128,8,96]{3,2,0,1:T(8,128)S(1)}, u32[]{:S(2)}, u32[]{:S(2)}) %all-to-all-start.1) | async-done | bytes 1572896 | tf_op jit(solution)/shard_map/all_to_all | solution.py:131
  137.2 1.5 copy.113
  138.7 2.3 %gather_fusion.3 = f32[254,8,96]{2,1,0:T(8,128)S(1)} fusion(f32[512,8,96]{2,1,0:T(8,128)} %bitcast.100, s32[1024]{0:T(1024)S(1)} %pad_clamp_fusion), kind=kCustom, calls=%fused_computation.3 | custom fusion | bytes 1561592 | tf_op jit(solution)/shard_map/jit(_take)/gather | solution.py:139
  142.5 3.1 %collective-permute-start = (f32[254,1,96]{2,1,0:T(1,128)}, f32[254,1,96]{2,1,0:T(1,128)S(1)}, u32[]{:S(2)}, u32[]{:S(2)}) collective-permute-start(f32[254,1,96]{2,1,0:T(1,128)} %get-tuple-element.218), channel_id=1, source_target_pairs={{16,0},{32,16},{48,32},{64,48},{80,64},{96,80},{112,96},{17,1},{33... | collective-permute-start | bytes 292616 | tf_op jit(solution)/shard_map/ppermute | solution.py:21
  145.6 2.5 %collective-permute-start.1 = (f32[254,1,96]{2,1,0:T(1,128)S(1)}, f32[254,1,96]{2,1,0:T(1,128)S(1)}, u32[]{:S(2)}, u32[]{:S(2)}) collective-permute-start(f32[254,1,96]{2,1,0:T(1,128)S(1)} %get-tuple-element.219), channel_id=1, source_target_pairs={{0,16},{16,32},{32,48},{48,64},{64,80},{80,96},{96,112},{1,17},{17... | collective-permute-start | bytes 292616 | tf_op jit(solution)/shard_map/ppermute | solution.py:18
  149.4 4.3 %collective-permute-start.2 = (f32[254,8,1]{0,1,2:T(8,128)S(1)}, f32[254,8,1]{0,1,2:T(8,128)S(1)}, u32[]{:S(2)}, u32[]{:S(2)}) collective-permute-start(f32[254,8,1]{0,1,2:T(8,128)S(1)} %copy.114), channel_id=1, source_target_pairs={{1,0},{2,1},{3,2},{4,3},{5,4},{6,5},{7,6},{8,7},{9,8},{10,9},{11,1... | collective-permute-start | bytes 24392 | tf_op jit(solution)/shard_map/ppermute | solution.py:21
  155.5 1.4 fusion.28
  157.2 1.3 copy.118
  (167 shorter events, 21.5 us)
Async XLA Ops:
  0.6 28.0 %copy-start = (f32[254,8]{0,1:T(8,128)S(1)}, f32[254,8]{0,1:T(8,128)}, u32[]{:S(2)}) copy-start(f32[254,8]{0,1:T(8,128)} %param.12) | copy-start | bytes 24388
  17.0 11.6 %copy-start.4 = (s32[64]{0:T(128)S(1)}, s32[64]{0:T(128)}, u32[]{:S(2)}) copy-start(s32[64]{0:T(128)} %param.14) | copy-start | bytes 772
  17.0 12.7 %copy-start.3 = (f32[254]{0:T(256)S(1)}, f32[254]{0:T(256)}, u32[]{:S(2)}) copy-start(f32[254]{0:T(256)} %param.13) | copy-start | bytes 3052
  17.0 41.2 %all-to-all-start = ((f32[4,128,8,96]{3,2,0,1:T(8,128)}), f32[4,128,8,96]{3,2,0,1:T(8,128)S(1)}, u32[]{:S(2)}, u32[]{:S(2)}) async-start(f32[4,128,8,96]{3,2,0,1:T(8,128)} %fusion.4), calls=%async_computation | async-start | bytes 4194304 | tf_op jit(solution)/shard_map/all_to_all | solution.py:112
  58.2 1.4 copy-start.1
  102.6 4.8 %copy-start.2 = (s32[254,1]{0,1:T(1,128)S(1)}, s32[254,1]{0,1:T(1,128)}, u32[]{:S(2)}) copy-start(s32[254,1]{0,1:T(1,128)} %param.15) | copy-start | bytes 3052
  102.6 34.6 %all-to-all-start.1 = ((f32[4,128,8,96]{3,2,0,1:T(8,128)}), f32[4,128,8,96]{3,2,0,1:T(8,128)S(1)}, u32[]{:S(2)}, u32[]{:S(2)}) async-start(f32[4,128,8,96]{3,2,0,1:T(8,128)} %copy.112), calls=%async_computation.1 | async-start | bytes 4194304 | tf_op jit(solution)/shard_map/all_to_all | solution.py:131
  142.5 12.9 %collective-permute-start = (f32[254,1,96]{2,1,0:T(1,128)}, f32[254,1,96]{2,1,0:T(1,128)S(1)}, u32[]{:S(2)}, u32[]{:S(2)}) collective-permute-start(f32[254,1,96]{2,1,0:T(1,128)} %get-tuple-element.218), channel_id=1, source_target_pairs={{16,0},{32,16},{48,32},{64,48},{80,64},{96,80},{112,96},{17,1},{33... | collective-permute-start | bytes 292616 | tf_op jit(solution)/shard_map/ppermute | solution.py:21
  145.6 9.9 %collective-permute-start.1 = (f32[254,1,96]{2,1,0:T(1,128)S(1)}, f32[254,1,96]{2,1,0:T(1,128)S(1)}, u32[]{:S(2)}, u32[]{:S(2)}) collective-permute-start(f32[254,1,96]{2,1,0:T(1,128)S(1)} %get-tuple-element.219), channel_id=1, source_target_pairs={{0,16},{16,32},{32,48},{48,64},{64,80},{80,96},{96,112},{1,17},{17... | collective-permute-start | bytes 292616 | tf_op jit(solution)/shard_map/ppermute | solution.py:18
  148.9 6.1 %collective-permute-start.3 = (f32[254,8,1]{0,1,2:T(8,128)S(1)}, f32[254,8,1]{0,1,2:T(8,128)S(1)}, u32[]{:S(2)}, u32[]{:S(2)}) collective-permute-start(f32[254,8,1]{0,1,2:T(8,128)S(1)} %copy.116), channel_id=1, source_target_pairs={{0,1},{1,2},{2,3},{3,4},{4,5},{5,6},{6,7},{7,8},{8,9},{9,10},{10,1... | collective-permute-start | bytes 24392 | tf_op jit(solution)/shard_map/ppermute | solution.py:18
  149.4 5.1 %collective-permute-start.2 = (f32[254,8,1]{0,1,2:T(8,128)S(1)}, f32[254,8,1]{0,1,2:T(8,128)S(1)}, u32[]{:S(2)}, u32[]{:S(2)}) collective-permute-start(f32[254,8,1]{0,1,2:T(8,128)S(1)} %copy.114), channel_id=1, source_target_pairs={{1,0},{2,1},{3,2},{4,3},{5,4},{6,5},{7,6},{8,7},{9,8},{10,9},{11,1... | collective-permute-start | bytes 24392 | tf_op jit(solution)/shard_map/ppermute | solution.py:21
where the time goes:
time: 159 us; the launch traced here: 158 us
  waiting for transfers between devices  56.1 us (35%)
  local copies, waits for them, and re-layouts  38.1 us (24%)
  starting transfers between devices  26.6 us (17%)
  matrix products  19.9 us (13%)
  other arithmetic  16.3 us (10%)
    all_to_all x1, waiting for transfers between devices, into_columns(): lax.all_to_all(pieces.reshape(most_slots, devices_all, latitude_points, l...  29.7 us
    all_to_all x1, waiting for transfers between devices, to_owners(): lax.all_to_all(packed.reshape(most_slots, devices_all, latitude_points, l...  25.6 us
    dot_general x2, matrix products, sweep_cols(): jnp.einsum('sbnm,swbm->swbn', transfer, parts, precision=HIGH_ACCURACY)  13.8 us
    all_to_all x1, starting transfers between devices, to_owners(): lax.all_to_all(packed.reshape(most_slots, devices_all, latitude_points, l...  11.5 us
    ppermute x2, starting transfers between devices, padded(): lax.ppermute(lax.slice_in_dim(block, 0, width, axis=dim), axis, backward)  7.38 us
    another operation x5, local copies, waits for them, and re-layouts  6.81 us
    all_to_all x1, starting transfers between devices, into_columns(): lax.all_to_all(pieces.reshape(most_slots, devices_all, latitude_points, l...  4.75 us
    dot_general x2, matrix products, sweep_rows(): jnp.einsum('sbnm,sbmw->sbnw', transfer, parts, precision=HIGH_ACCURACY)  4.42 us
  transfers between devices with their start and end apart: 6, of which 3 were waited for; matrix products, arithmetic and copies ran while one was open for 4% of the time, Pallas kernels for 0%

commit v1 on v0

--- a/solution.py
+++ b/solution.py
@@ -109,12 +109,20 @@
     by_slot = source.reshape(devices_all, most_slots).T.reshape(-1)
     live_slot = filled.reshape(devices_all, most_slots).T.reshape(-1)
     packed = jnp.where(live_slot[:, None, None], jnp.take(columns, by_slot, axis=0), 0.0)
-    moved = lax.all_to_all(
-        packed.reshape(most_slots, devices_all, latitude_points, longitude_points),
-        ("lat", "lon"),
-        split_axis=1,
-        concat_axis=1,
-        tiled=True,
+    moved = jnp.concatenate(
+        lax.all_to_all(
+            jnp.stack(
+                jnp.split(
+                    packed.reshape(most_slots, devices_all, latitude_points, longitude_points),
+                    lax.axis_size(("lat", "lon")),
+                    axis=1,
+                )
+            ),
+            ("lat", "lon"),
+            0,
+            0,
+        ),
+        axis=1,
     )
     moved = moved.reshape(most_slots, lat_count, lon_count, latitude_points, longitude_points)
     return moved.transpose(0, 1, 3, 2, 4).reshape(

time: 159 us -> 239 us (1.50)
  local copies, waits for them, and re-layouts: 38.1 us -> 118 us
    unnamed x13 -> x140, local copies, waits for them, and re-layouts: 3.57 us -> 79.8 us
    rev x1, local copies, waits for them, and re-layouts: 1.45 us -> 4.78 us  [filter_slabs(): jnp.flip(eastward, 2)]
    another operation x5 -> x6, local copies, waits for them, and re-layouts: 6.81 us -> 7.42 us
  transfers between devices with their start and end apart: 6 -> 6, of which waited for: 3 -> 3; matrix products, arithmetic and copies ran while one was open for 4% -> 2% of each run, Pallas kernels for 0% -> 0%
where the time goes in v1:
time: 239 us
  local copies, waits for them, and re-layouts  118 us (49%)
  waiting for transfers between devices  56.2 us (24%)
  starting transfers between devices  26.6 us (11%)
  matrix products  21.3 us (9%)
  other arithmetic  14.7 us (6%)
    unnamed x140, local copies, waits for them, and re-layouts  79.8 us
    all_to_all x1, waiting for transfers between devices, into_columns(): lax.all_to_all(pieces.reshape(most_slots, devices_all, latitude_points, l...  29.7 us
    all_to_all x1, waiting for transfers between devices, to_owners(): lax.all_to_all(jnp.stack(jnp.split(packed.reshape(most_slots, devices_all...  25.7 us
    dot_general x2, matrix products, sweep_cols(): jnp.einsum('sbnm,swbm->swbn', transfer, parts, precision=HIGH_ACCURACY)  15.1 us
    all_to_all x1, starting transfers between devices, to_owners(): lax.all_to_all(jnp.stack(jnp.split(packed.reshape(most_slots, devices_all...  11.5 us
    ppermute x2, starting transfers between devices, padded(): lax.ppermute(lax.slice_in_dim(block, 0, width, axis=dim), axis, backward)  7.38 us
    another operation x5, local copies, waits for them, and re-layouts  6.81 us
  transfers between devices with their start and end apart: 6, of which 3 were waited for; matrix products, arithmetic and copies ran while one was open for 2% of the time, Pallas kernels for 0%

profile of v1, /device:TPU:1, one launch (start us, length us, event | category | flops | bytes accessed | tf_op | source)
XLA Modules:
  0.0 238.6 jit_solution(17321922456233702022)
XLA Ops:
  0.7 0.9 convert_reduce_fusion
  5.1 1.7 reshape.571
  7.8 2.8 %stack.402 = pred[9,127,127]{2,0,1:T(8,128)(4,1)S(1)} concatenate(pred[1,127,127]{2,0,1:T(4,128)(4,1)S(1)} %iota_compare_fusion.12, pred[1,127,127]{2,0,1:T(4,128)(4,1)S(1)} %get-tuple-element.237, pred[1,127,127]{2,0,1:T(4,128)(4,1)S(1)} %get-tuple-element.236, pred[1,127,127]{2,0,1:T(4,128)(4,1)S(1)} %get-tuple-element.235, pred[1,127,127]{2,0,1:T(4,128)(4,1)S(1)} %get-tuple-element.234, ...), dimensions={0} | concatenate | bytes 290322 | tf_op jit(solution)/shard_map/stack | solution.py:180
  12.6 1.9 gather_fusion.1
  14.5 1.1 fusion.4
  92.5 11.5 %all-to-all-start = ((f32[128,4,1,8,96]{4,3,1,2,0:T(8,128)}), f32[128,4,1,8,96]{4,3,1,2,0:T(8,128)S(1)}, u32[]{:S(2)}, u32[]{:S(2)}) async-start(f32[128,4,1,8,96]{4,3,1,2,0:T(8,128)} %constant_dynamic-update-slice_fusion), calls=%async_computation | async-start | bytes 4194304 | tf_op jit(solution)/shard_map/all_to_all | solution.py:113
  105.9 1.1 reduce_window_sum.30
  108.0 25.7 %all-to-all-done = f32[128,4,1,8,96]{4,3,1,2,0:T(8,128)S(1)} async-done(((f32[128,4,1,8,96]{4,3,1,2,0:T(8,128)}), f32[128,4,1,8,96]{4,3,1,2,0:T(8,128)S(1)}, u32[]{:S(2)}, u32[]{:S(2)}) %all-to-all-start) | async-done | bytes 1572896 | tf_op jit(solution)/shard_map/all_to_all | solution.py:113
  133.7 1.3 copy-done.1
  135.0 2.8 %copy.354 = f32[4,8,8,16,96]{4,3,2,1,0:T(8,128)S(1)} copy(f32[4,8,8,16,96]{4,2,0,3,1:T(8,128)} %bitcast.611) | data formatting | bytes 3145728 | tf_op jit(solution)/shard_map/transpose | solution.py:128
  137.9 2.1 reshape.575
  140.0 2.9 %convolution_add_fusion.1 = f32[4,64,1536]{2,1,0:T(8,128)S(1)} fusion(f32[4,64,1536]{2,1,0:T(8,128)} %reshape.575, f32[4,64]{1,0:T(4,128)S(1)} %exponential_multiply_fusion.1, f32[4,64]{1,0:T(4,128)S(1)} %get-tuple-element.208, f32[4,64]{1,0:T(4,128)S(1)} %reduce_window_sum.29, pred[64,64]{1,0:T(8,128)(4,1)S(1)} %iota_compare_fusion.13), kind=kOutput, calls=%fused_computation.16 | convolution fusion | flops 302448640 | bytes 3152896 | tf_op jit(solution)/shard_map/sbnm,sbmw->sbnw/dot_general | solution.py:67
  143.4 1.5 convolution_add_fusion
  144.9 4.2 %reverse.8 = f32[4,64,1536]{2,1,0:T(8,128)} reverse(f32[4,64,1536]{2,1,0:T(8,128)S(1)} %convolution_add_fusion), dimensions={1} | reverse | bytes 3145728 | tf_op jit(solution)/shard_map/reverse.2
  149.1 7.6 %fusion.19 = f32[4,64,12,128]{3,1,2,0:T(8,128)S(1)} fusion(f32[4]{0:T(128)S(1)} %get-tuple-element.227, f32[4,12,128]{2,1,0:T(8,128)S(1)} %reduce_window_sum.30, pred[128,128]{1,0:T(8,128)(4,1)S(1)} %iota_compare_fusion.2, f32[4,64,1536]{2,1,0:T(8,128)} %reverse.8), kind=kOutput, calls=%fused_computation.39 | convolution fusion | flops 607125504 | bytes 3186704 | tf_op jit(solution)/shard_map/sbnm,swbm->swbn/dot_general | solution.py:77
  157.7 1.4 while.6
  160.3 4.8 %rev.15 = f32[4,64,1536]{2,1,0:T(8,128)} reverse(f32[4,64,1536]{2,1,0:T(8,128)S(1)} %multiply_add_fusion.1), dimensions={2} | reverse | bytes 3145728 | tf_op jit(solution)/shard_map/jit(_flip)/rev | solution.py:99
  165.1 7.6 %fusion.22 = f32[4,64,12,128]{3,1,2,0:T(8,128)S(1)} fusion(f32[4]{0:T(128)S(1)} %get-tuple-element.227, f32[4,12,128]{2,1,0:T(8,128)S(1)} %reduce_window_sum.30, pred[128,128]{1,0:T(8,128)(4,1)S(1)} %iota_compare_fusion.2, f32[4,64,1536]{2,1,0:T(8,128)} %rev.15), kind=kOutput, calls=%fused_computation.40 | convolution fusion | flops 607125504 | bytes 3186704 | tf_op jit(solution)/shard_map/sbnm,swbm->swbn/dot_general | solution.py:77
  173.7 1.2 while.7
  175.5 1.4 rev.16
  177.0 1.4 multiply_add_fusion
  178.3 1.9 reshape.581
  181.2 1.6 copy.366
  182.8 4.8 %all-to-all-start.1 = ((f32[4,128,8,96]{3,2,0,1:T(8,128)}), f32[4,128,8,96]{3,2,0,1:T(8,128)S(1)}, u32[]{:S(2)}, u32[]{:S(2)}) async-start(f32[4,128,8,96]{3,2,0,1:T(8,128)} %copy.366), calls=%async_computation.1 | async-start | bytes 4194304 | tf_op jit(solution)/shard_map/all_to_all | solution.py:139
  187.6 29.7 %all-to-all-done.1 = f32[4,128,8,96]{3,2,0,1:T(8,128)S(1)} async-done(((f32[4,128,8,96]{3,2,0,1:T(8,128)}), f32[4,128,8,96]{3,2,0,1:T(8,128)S(1)}, u32[]{:S(2)}, u32[]{:S(2)}) %all-to-all-start.1) | async-done | bytes 1572896 | tf_op jit(solution)/shard_map/all_to_all | solution.py:139
  217.4 1.5 copy.367
  218.9 2.3 gather_fusion.3
  222.7 3.1 %collective-permute-start = (f32[254,1,96]{2,1,0:T(1,128)}, f32[254,1,96]{2,1,0:T(1,128)S(1)}, u32[]{:S(2)}, u32[]{:S(2)}) collective-permute-start(f32[254,1,96]{2,1,0:T(1,128)} %get-tuple-element.218), channel_id=1, source_target_pairs={{16,0},{32,16},{48,32},{64,48},{80,64},{96,80},{112,96},{17,1},{33... | collective-permute-start | bytes 292616 | tf_op jit(solution)/shard_map/ppermute | solution.py:21
  225.8 2.5 %collective-permute-start.1 = (f32[254,1,96]{2,1,0:T(1,128)S(1)}, f32[254,1,96]{2,1,0:T(1,128)S(1)}, u32[]{:S(2)}, u32[]{:S(2)}) collective-permute-start(f32[254,1,96]{2,1,0:T(1,128)S(1)} %get-tuple-element.219), channel_id=1, source_target_pairs={{0,16},{16,32},{32,48},{48,64},{64,80},{80,96},{96,112},{1,17},{17... | collective-permute-start | bytes 292616 | tf_op jit(solution)/shard_map/ppermute | solution.py:18
  229.6 4.3 %collective-permute-start.2 = (f32[254,8,1]{0,1,2:T(8,128)S(1)}, f32[254,8,1]{0,1,2:T(8,128)S(1)}, u32[]{:S(2)}, u32[]{:S(2)}) collective-permute-start(f32[254,8,1]{0,1,2:T(8,128)S(1)} %copy.368), channel_id=1, source_target_pairs={{1,0},{2,1},{3,2},{4,3},{5,4},{6,5},{7,6},{8,7},{9,8},{10,9},{11,1... | collective-permute-start | bytes 24392 | tf_op jit(solution)/shard_map/ppermute | solution.py:21
  235.7 1.4 fusion.28
  237.3 1.3 copy.372
  (294 shorter events, 98.3 us)
Async XLA Ops:
  0.6 103.4 %copy-start = (f32[254,8]{0,1:T(8,128)S(1)}, f32[254,8]{0,1:T(8,128)}, u32[]{:S(2)}) copy-start(f32[254,8]{0,1:T(8,128)} %param.12) | copy-start | bytes 24388
  92.5 11.5 %copy-start.4 = (s32[64]{0:T(128)S(1)}, s32[64]{0:T(128)}, u32[]{:S(2)}) copy-start(s32[64]{0:T(128)} %param.14) | copy-start | bytes 772
  92.5 12.6 %copy-start.3 = (f32[254]{0:T(256)S(1)}, f32[254]{0:T(256)}, u32[]{:S(2)}) copy-start(f32[254]{0:T(256)} %param.13) | copy-start | bytes 3052
  92.5 41.2 %all-to-all-start = ((f32[128,4,1,8,96]{4,3,1,2,0:T(8,128)}), f32[128,4,1,8,96]{4,3,1,2,0:T(8,128)S(1)}, u32[]{:S(2)}, u32[]{:S(2)}) async-start(f32[128,4,1,8,96]{4,3,1,2,0:T(8,128)} %constant_dynamic-update-slice_fusion), calls=%async_computation | async-start | bytes 4194304 | tf_op jit(solution)/shard_map/all_to_all | solution.py:113
  133.7 1.4 copy-start.1
  182.8 4.8 %copy-start.2 = (s32[254,1]{0,1:T(1,128)S(1)}, s32[254,1]{0,1:T(1,128)}, u32[]{:S(2)}) copy-start(s32[254,1]{0,1:T(1,128)} %param.15) | copy-start | bytes 3052
  182.8 34.6 %all-to-all-start.1 = ((f32[4,128,8,96]{3,2,0,1:T(8,128)}), f32[4,128,8,96]{3,2,0,1:T(8,128)S(1)}, u32[]{:S(2)}, u32[]{:S(2)}) async-start(f32[4,128,8,96]{3,2,0,1:T(8,128)} %copy.366), calls=%async_computation.1 | async-start | bytes 4194304 | tf_op jit(solution)/shard_map/all_to_all | solution.py:139
  222.7 12.9 %collective-permute-start = (f32[254,1,96]{2,1,0:T(1,128)}, f32[254,1,96]{2,1,0:T(1,128)S(1)}, u32[]{:S(2)}, u32[]{:S(2)}) collective-permute-start(f32[254,1,96]{2,1,0:T(1,128)} %get-tuple-element.218), channel_id=1, source_target_pairs={{16,0},{32,16},{48,32},{64,48},{80,64},{96,80},{112,96},{17,1},{33... | collective-permute-start | bytes 292616 | tf_op jit(solution)/shard_map/ppermute | solution.py:21
  225.8 9.9 %collective-permute-start.1 = (f32[254,1,96]{2,1,0:T(1,128)S(1)}, f32[254,1,96]{2,1,0:T(1,128)S(1)}, u32[]{:S(2)}, u32[]{:S(2)}) collective-permute-start(f32[254,1,96]{2,1,0:T(1,128)S(1)} %get-tuple-element.219), channel_id=1, source_target_pairs={{0,16},{16,32},{32,48},{48,64},{64,80},{80,96},{96,112},{1,17},{17... | collective-permute-start | bytes 292616 | tf_op jit(solution)/shard_map/ppermute | solution.py:18
  229.1 6.1 %collective-permute-start.3 = (f32[254,8,1]{0,1,2:T(8,128)S(1)}, f32[254,8,1]{0,1,2:T(8,128)S(1)}, u32[]{:S(2)}, u32[]{:S(2)}) collective-permute-start(f32[254,8,1]{0,1,2:T(8,128)S(1)} %copy.370), channel_id=1, source_target_pairs={{0,1},{1,2},{2,3},{3,4},{4,5},{5,6},{6,7},{7,8},{8,9},{9,10},{10,1... | collective-permute-start | bytes 24392 | tf_op jit(solution)/shard_map/ppermute | solution.py:18
  229.6 5.1 %collective-permute-start.2 = (f32[254,8,1]{0,1,2:T(8,128)S(1)}, f32[254,8,1]{0,1,2:T(8,128)S(1)}, u32[]{:S(2)}, u32[]{:S(2)}) collective-permute-start(f32[254,8,1]{0,1,2:T(8,128)S(1)} %copy.368), channel_id=1, source_target_pairs={{1,0},{2,1},{3,2},{4,3},{5,4},{6,5},{7,6},{8,7},{9,8},{10,9},{11,1... | collective-permute-start | bytes 24392 | tf_op jit(solution)/shard_map/ppermute | solution.py:21
